TPU v7x, 32 devices: a whole 2x2x4 slice. The times are simulated.
32 devices in a mesh: blk: 8 (over y, x, core), red: 4 (over z).
Axes of the slice: x: 2, y: 2, z: 4, core: 2. Of those that a mesh axis runs over, the one named last changes fastest.
Arguments:
- x_now: bfloat16 [512, 131072], P('blk', 'red'), may hold values from -6 to 6
- x_prev: float32 [512, 131072], P('blk', 'red'), may hold values from -6 to 6
- density: float32 [512, 131072], P('blk', 'red'), may hold values from -6 to 6
- coeffs: float32 [8], replicated, may hold values from -1 to 1
- potential: int32 [32], P('blk'), may hold values from 0 to 7
- h_tiles: bfloat16 [8, 48, 256, 256], P('blk', 'red'), may hold values from -0.1796875 to 0.1796875
- tile_rows: int32 [8, 48], P('blk', 'red'), may hold values from 0 to 63
- tile_cols: int32 [8, 48], P('blk', 'red'), may hold values from 0 to 127, as said below
- tile_counts: int32 [8, 4], P('blk', 'red'), may hold values from 3 to 12, as said below
Outputs:
- x_next: float32 [512, 131072], P('blk', 'red')
- density_out: float32 [512, 131072], P('blk', 'red')
Inputs may be any that keep to these rules, and one draw needn't show every extreme that they name: `tile_cols`: block column within the group; the live slots of one panel and group name distinct positions (row, column). `tile_counts`: at most 12 live slots; some panel and group is full in every draw.
All inputs are finite; a program needn't handle non-finite values.
Results may differ from a plain program's by a relative error of at most 0.005.
Values may be sent and summed in bfloat16 or wider, within the bound.
No kernel may reach another device: no remote copies, remote signals or barrier semaphores. Data moves between devices by JAX's collectives and lax.ppermute only.
A program may use at most 128 MiB of HBM per device.

v0:
```python
import jax
import jax.numpy as jnp
from jax import lax
from jax.sharding import PartitionSpec as P


def for_sending(x):

    def short(part):
        return part.astype(jnp.bfloat16) if part.dtype == jnp.float32 else part

    return jax.tree.map(short, x)


def from_behind(value, axis, steps):
    count = lax.axis_size(axis)
    pairs = [(source, (source + steps) % count) for source in range(count)]
    return lax.ppermute(value, axis, pairs)


def shards(x_now, x_prev, density, coeffs, potential, h_tiles, tile_rows, tile_cols, tile_counts):
    columns, local_rows = x_now.shape
    blk_count = lax.axis_size("blk")
    red_count = lax.axis_size("red")
    tile_width = h_tiles.shape[-1]
    capacity = h_tiles.shape[1]
    col_blocks = local_rows // tile_width
    row_blocks = local_rows * red_count // tile_width // blk_count
    owned_panels = blk_count // red_count
    x_blocks = x_now.reshape(columns, col_blocks, tile_width)
    anchor = lax.axis_index("blk")
    slot_index = jnp.arange(capacity, dtype=jnp.int32)

    def slot_products(state):
        tile_data, row_ids, col_ids, live_count = state
        picked = jnp.take(x_blocks, col_ids, axis=1)
        product = jnp.einsum("vck,cik->cvi", picked, tile_data, preferred_element_type=jnp.float32)
        is_live = slot_index < live_count
        return (product, row_ids, is_live)

    def packed_rows(state):
        product, row_ids, is_live = slot_products(state)
        same_row = (row_ids[:, None] == row_ids[None, :]) & is_live[:, None] & is_live[None, :]
        before = same_row & (slot_index[None, :] < slot_index[:, None])
        leading = is_live & jnp.logical_not(jnp.any(before, axis=1))
        collect = (same_row & leading[:, None]).astype(jnp.float32)
        summed = jnp.einsum("st,tvi->vsi", collect, product, precision=lax.Precision.HIGHEST)
        values = summed.reshape(columns, 1, capacity * tile_width).astype(jnp.bfloat16)
        numbers = (
            jnp.where(leading, row_ids, -1)
            .astype(jnp.float32)
            .astype(jnp.bfloat16)
            .reshape(1, capacity)
        )
        return (values, numbers)

    holder = (
        jnp.zeros((columns, blk_count, capacity * tile_width), jnp.bfloat16),
        jnp.full((blk_count, capacity), -1.0, jnp.bfloat16),
    )

    def place(totals, state, panel_index):
        where_at = jnp.asarray(panel_index % blk_count, dtype=jnp.int32)
        values, numbers = packed_rows(state)
        stored = lax.dynamic_update_slice_in_dim(totals[0], values, where_at, 1)
        labels = lax.dynamic_update_slice_in_dim(totals[1], numbers, where_at, 0)
        return (stored, labels)

    start_state = (h_tiles[0], tile_rows[0], tile_cols[0], tile_counts[0, 0])
    totals = holder

    def advance(number, carry):
        state, partial_sums = carry
        partial_sums = place(partial_sums, state, anchor - number)
        state = jax.tree.map(
            lambda part, own: part.astype(own.dtype),
            from_behind(for_sending(state), "blk", 1),
            state,
        )
        return (state, partial_sums)

    last_state, totals = lax.fori_loop(0, blk_count - 1, advance, (start_state, totals))
    totals = place(totals, last_state, anchor - (blk_count - 1))
    stored, labels = totals
    stored = stored.reshape(columns, blk_count, 1, capacity * tile_width)
    labels = labels.reshape(1, blk_count, 1, capacity)
    arrived, arrived_labels = (
        lax.all_to_all(stored, "red", split_axis=1, concat_axis=2, tiled=True),
        lax.all_to_all(labels, "red", split_axis=1, concat_axis=2, tiled=True),
    )
    arrived = arrived.reshape(columns, owned_panels, red_count, capacity, tile_width)
    targets = jnp.arange(row_blocks, dtype=jnp.int32).astype(jnp.float32)
    placing = (
        arrived_labels.reshape(owned_panels, red_count, capacity)[:, :, :, None].astype(jnp.float32)
        == targets[None, None, None, :]
    ).astype(jnp.bfloat16)
    gathered = jnp.einsum("prsq,vprsi->vpqi", placing, arrived, preferred_element_type=jnp.float32)
    product = gathered.reshape(columns, local_rows)
    x_next = 2.0 * product - x_prev
    slabs_here = potential.shape[0]
    slab_width = columns // slabs_here
    picking = (potential[:, None] == jnp.arange(coeffs.shape[0], dtype=jnp.int32)[None, :]).astype(
        jnp.float32
    )
    slab_coef = jnp.sum(picking * coeffs[None, :], axis=1)
    column_coef = jnp.repeat(slab_coef, slab_width)
    density_out = density + column_coef[:, None] * x_next
    return (x_next, density_out)


def solution(mesh):
    in_specs = (
        P("blk", "red"),
        P("blk", "red"),
        P("blk", "red"),
        P(),
        P("blk"),
        P("blk", "red", None, None),
        P("blk", "red"),
        P("blk", "red"),
        P("blk", "red"),
    )
    out_specs = (P("blk", "red"), P("blk", "red"))
    return jax.shard_map(shards, mesh=mesh, in_specs=in_specs, out_specs=out_specs, check_vma=False)
```

profile of v0, /device:TPU:0, one launch (start us, length us, event | category | flops | bytes accessed | tf_op | source)
XLA Modules:
  0.0 306.0 jit_solution(4496815559628200654)
XLA Ops:
  3.7 4.9 %copy.73 = bf16[8,128,8,256]{3,2,0,1:T(8,128)(2,1)} copy(bf16[8,128,8,256]{3,2,1,0:T(8,128)(2,1)} %bitcast.76) | data formatting | bytes 8388608 | tf_op jit(solution)/shard_map/reshape | solution.py:30
  9.2 2.0 broadcast_in_dim.64
  11.2 179.1 %while.27 = (s32[]{:T(128)}, bf16[12,256,256]{2,1,0:T(8,128)(2,1)S(1)}, s32[12]{0:T(128)}, s32[12]{0:T(128)}, s32[]{:T(128)}, /*index=5*/bf16[64,8,3072]{2,0,1:T...) while((s32[]{:T(128)}, ...), condition=%wide.region_2.4_spmd.clone.clone, body=%wide.region_0.3_spmd.clone.clone.sunk | while | flops 129370712 | bytes 15734480 | solution.py:82
  13.5 2.6 collective-permute-start.1
  17.2 1.4 collective-permute-start
  19.9 2.8 gather_fusion
  23.9 2.0 fusion.56
  25.9 1.3 convert_element_type.139
  29.3 8.7 %collective-permute-done = bf16[12,256,256]{2,1,0:T(8,128)(2,1)S(1)} collective-permute-done((bf16[12,256,256]{2,1,0:T(8,128)(2,1)S(1)}, bf16[12,256,256]{2,1,0:T(8,128)(2,1)S(1)}, u32[]{:S(2)}, u32[]{:S(2)}) %collective-permute-start) | collective-permute-done | bytes 1572896 | tf_op jit(solution)/shard_map/while/body/eval_jaxpr/ppermute | solution.py:18
  42.2 2.3 collective-permute-start
  45.8 2.8 gather_fusion
  49.8 2.0 fusion.56
  51.8 1.3 convert_element_type.139
  55.2 7.8 %collective-permute-done = bf16[12,256,256]{2,1,0:T(8,128)(2,1)S(1)} collective-permute-done((bf16[12,256,256]{2,1,0:T(8,128)(2,1)S(1)}, bf16[12,256,256]{2,1,0:T(8,128)(2,1)S(1)}, u32[]{:S(2)}, u32[]{:S(2)}) %collective-permute-start) | collective-permute-done | bytes 1572896 | tf_op jit(solution)/shard_map/while/body/eval_jaxpr/ppermute | solution.py:18
  65.4 1.6 collective-permute-start.1
  70.1 2.8 gather_fusion
  74.1 2.0 fusion.56
  76.1 1.3 convert_element_type.139
  79.5 9.4 %collective-permute-done = bf16[12,256,256]{2,1,0:T(8,128)(2,1)S(1)} collective-permute-done((bf16[12,256,256]{2,1,0:T(8,128)(2,1)S(1)}, bf16[12,256,256]{2,1,0:T(8,128)(2,1)S(1)}, u32[]{:S(2)}, u32[]{:S(2)}) %collective-permute-start) | collective-permute-done | bytes 1572896 | tf_op jit(solution)/shard_map/while/body/eval_jaxpr/ppermute | solution.py:18
  92.4 2.0 collective-permute-start
  95.7 2.8 gather_fusion
  99.7 2.0 fusion.56
  101.7 1.3 convert_element_type.139
  105.1 8.1 %collective-permute-done = bf16[12,256,256]{2,1,0:T(8,128)(2,1)S(1)} collective-permute-done((bf16[12,256,256]{2,1,0:T(8,128)(2,1)S(1)}, bf16[12,256,256]{2,1,0:T(8,128)(2,1)S(1)}, u32[]{:S(2)}, u32[]{:S(2)}) %collective-permute-start) | collective-permute-done | bytes 1572896 | tf_op jit(solution)/shard_map/while/body/eval_jaxpr/ppermute | solution.py:18
  118.0 1.4 collective-permute-start
  120.7 2.8 gather_fusion
  124.7 2.0 fusion.56
  126.7 1.3 convert_element_type.139
  130.1 8.7 %collective-permute-done = bf16[12,256,256]{2,1,0:T(8,128)(2,1)S(1)} collective-permute-done((bf16[12,256,256]{2,1,0:T(8,128)(2,1)S(1)}, bf16[12,256,256]{2,1,0:T(8,128)(2,1)S(1)}, u32[]{:S(2)}, u32[]{:S(2)}) %collective-permute-start) | collective-permute-done | bytes 1572896 | tf_op jit(solution)/shard_map/while/body/eval_jaxpr/ppermute | solution.py:18
  143.0 2.3 collective-permute-start
  146.6 2.8 gather_fusion
  150.6 2.0 fusion.56
  156.0 7.8 %collective-permute-done = bf16[12,256,256]{2,1,0:T(8,128)(2,1)S(1)} collective-permute-done((bf16[12,256,256]{2,1,0:T(8,128)(2,1)S(1)}, bf16[12,256,256]{2,1,0:T(8,128)(2,1)S(1)}, u32[]{:S(2)}, u32[]{:S(2)}) %collective-permute-start) | collective-permute-done | bytes 1572896 | tf_op jit(solution)/shard_map/while/body/eval_jaxpr/ppermute | solution.py:18
  166.2 1.6 collective-permute-start.1
  170.9 2.8 gather_fusion
  174.9 2.0 fusion.56
  180.3 9.4 %collective-permute-done = bf16[12,256,256]{2,1,0:T(8,128)(2,1)S(1)} collective-permute-done((bf16[12,256,256]{2,1,0:T(8,128)(2,1)S(1)}, bf16[12,256,256]{2,1,0:T(8,128)(2,1)S(1)}, u32[]{:S(2)}, u32[]{:S(2)}) %collective-permute-start) | collective-permute-done | bytes 1572896 | tf_op jit(solution)/shard_map/while/body/eval_jaxpr/ppermute | solution.py:18
  194.4 4.9 %all-to-all-start.1 = ((bf16[1,8,1,12]{3,2,0,1:T(2,128)(2,1)}), bf16[1,8,1,12]{3,2,0,1:T(2,128)(2,1)S(1)}, u32[]{:S(2)}, u32[]{:S(2)}) async-start(bf16[1,8,1,12]{3,2,0,1:T(2,128)(2,1)} %copy.49), calls=%async_computation.1 | async-start | bytes 8192 | tf_op jit(solution)/shard_map/all_to_all | solution.py:89
  200.0 2.8 gather_fusion.1
  203.4 1.9 fusion.23
  206.4 5.1 %all-to-all-start = ((bf16[64,8,1,3072]{3,0,2,1:T(8,128)(2,1)}), bf16[64,8,1,3072]{3,0,2,1:T(8,128)(2,1)S(1)}, u32[]{:S(2)}, u32[]{:S(2)}) async-start(bf16[64,8,1,3072]{3,0,2,1:T(8,128)(2,1)} %constant_dynamic-update-slice_fusion.1), calls=%async_computation | async-start | bytes 6291456 | tf_op jit(solution)/shard_map/all_to_all | solution.py:88
  211.8 67.4 %all-to-all-done = bf16[64,8,1,3072]{3,0,2,1:T(8,128)(2,1)S(1)} async-done(((bf16[64,8,1,3072]{3,0,2,1:T(8,128)(2,1)}), bf16[64,8,1,3072]{3,0,2,1:T(8,128)(2,1)S(1)}, u32[]{:S(2)}, u32[]{:S(2)}) %all-to-all-start) | async-done | bytes 3145760 | tf_op jit(solution)/shard_map/all_to_all | solution.py:88
  279.3 1.7 copy-done.1
  280.9 2.2 copy.74
  283.1 3.5 %reshape.144 = bf16[64,2,4,12,256]{4,3,0,2,1:T(8,128)(2,1)} reshape(bf16[64,2,4,1,3072]{4,0,2,1,3:T(8,128)(2,1)S(1)} %bitcast.73) | data formatting | bytes 6291456 | tf_op jit(solution)/shard_map/reshape | solution.py:91
  286.7 3.6 %bitcast_multiply_fusion = f32[2,64,256,64]{2,3,0,1:T(8,128)S(1)} fusion(bf16[64,2,4,12,256]{4,3,0,2,1:T(8,128)(2,1)} %reshape.144, f32[64]{0:T(128)S(1)} %iota_convert_fusion, f32[2,4,12]{2,0,1:T(2,128)S(1)} %convert_bitcast_fusion.1), kind=kOutput, calls=%fused_computation.30 | convolution fusion | flops 203429888 | bytes 11534976 | tf_op jit(solution)/shard_map/prsq,vprsi->vpqi/dot_general | solution.py:97
  290.2 4.7 %copy.60 = f32[8,8,128,256]{3,1,2,0:T(8,128)S(1)} copy(f32[8,8,128,256]{3,2,1,0:T(8,128)S(1)} %bitcast.70) | data formatting | bytes 16777216
  295.0 11.1 %multiply_add_fusion = (f32[64,32768]{1,0:T(8,128)}, f32[64,32768]{1,0:T(8,128)}) fusion(f32[64,32768]{1,0:T(8,128)} %param.15, f32[64]{0:T(128)S(1)} %mul.36, f32[64,32768]{1,0:T(8,128)S(1)} %bitcast.71, f32[64,32768]{1,0:T(8,128)} %param.14), kind=kLoop, calls=%fused_computation.31 | loop fusion | flops 6291456 | bytes 41943296 | tf_op jit(solution)/shard_map/add | solution.py:107
  (161 shorter events, 69.0 us)
Async XLA Ops:
  3.7 7.5 %copy-start = (bf16[1,12,256,256]{3,2,1,0:T(8,128)(2,1)S(1)}, bf16[1,12,256,256]{3,2,1,0:T(8,128)(2,1)}, u32[]{:S(2)}) copy-start(bf16[1,12,256,256]{3,2,1,0:T(8,128)(2,1)} %param.18) | copy-start | bytes 4718596
  12.4 16.9 %collective-permute-start.2 = (s32[12]{0:T(128)}, s32[12]{0:T(128)}, u32[]{:S(2)}, u32[]{:S(2)}) collective-permute-start(s32[12]{0:T(128)} %copy.89), channel_id=1, source_target_pairs={{0,4},{4,8},{8,12},{12,16},{16,20},{20,24},{24,28},{28,0},{1,5},{5... | collective-permute-start | bytes 152 | tf_op jit(solution)/shard_map/while/body/eval_jaxpr/ppermute | solution.py:18
  13.5 15.8 %collective-permute-start.1 = (s32[12]{0:T(128)S(1)}, s32[12]{0:T(128)}, u32[]{:S(2)}, u32[]{:S(2)}) collective-permute-start(s32[12]{0:T(128)S(1)} %copy.88), channel_id=1, source_target_pairs={{0,4},{4,8},{8,12},{12,16},{16,20},{20,24},{24,28},{28,0},{1,5},{5... | collective-permute-start | bytes 152 | tf_op jit(solution)/shard_map/while/body/eval_jaxpr/ppermute | solution.py:18
  16.1 13.2 %collective-permute-start.3 = (s32[]{:T(128)}, s32[]{:T(128)}, u32[]{:S(2)}, u32[]{:S(2)}) collective-permute-start(s32[]{:T(128)} %copy.90), channel_id=1, source_target_pairs={{0,4},{4,8},{8,12},{12,16},{16,20},{20,24},{24,28},{28,0},{1,5},{5... | collective-permute-start | bytes 20 | tf_op jit(solution)/shard_map/while/body/eval_jaxpr/ppermute | solution.py:18
  17.2 20.8 %collective-permute-start = (bf16[12,256,256]{2,1,0:T(8,128)(2,1)S(1)}, bf16[12,256,256]{2,1,0:T(8,128)(2,1)S(1)}, u32[]{:S(2)}, u32[]{:S(2)}) collective-permute-start(bf16[12,256,256]{2,1,0:T(8,128)(2,1)S(1)} %copy.87), channel_id=1, source_target_pairs={{0,4},{4,8},{8,12},{12,16},{16,20},{20,24},{24,28},{28,0},{1,5},{5... | collective-permute-start | bytes 4718600 | tf_op jit(solution)/shard_map/while/body/eval_jaxpr/ppermute | solution.py:18
  22.7 4.6 %copy-start.2 = (bf16[1,12]{1,0:T(2,128)(2,1)S(1)}, bf16[1,12]{1,0:T(2,128)(2,1)}, u32[]{:S(2)}) copy-start(bf16[1,12]{1,0:T(2,128)(2,1)} %get-tuple-element.417) | copy-start | bytes 76 | tf_op jit(solution)/shard_map/while
  39.8 15.4 %collective-permute-start.2 = (s32[12]{0:T(128)}, s32[12]{0:T(128)}, u32[]{:S(2)}, u32[]{:S(2)}) collective-permute-start(s32[12]{0:T(128)} %copy.89), channel_id=1, source_target_pairs={{0,4},{4,8},{8,12},{12,16},{16,20},{20,24},{24,28},{28,0},{1,5},{5... | collective-permute-start | bytes 152 | tf_op jit(solution)/shard_map/while/body/eval_jaxpr/ppermute | solution.py:18
  40.4 14.8 %collective-permute-start.1 = (s32[12]{0:T(128)S(1)}, s32[12]{0:T(128)}, u32[]{:S(2)}, u32[]{:S(2)}) collective-permute-start(s32[12]{0:T(128)S(1)} %copy.88), channel_id=1, source_target_pairs={{0,4},{4,8},{8,12},{12,16},{16,20},{20,24},{24,28},{28,0},{1,5},{5... | collective-permute-start | bytes 152 | tf_op jit(solution)/shard_map/while/body/eval_jaxpr/ppermute | solution.py:18
  41.1 14.1 %collective-permute-start.3 = (s32[]{:T(128)}, s32[]{:T(128)}, u32[]{:S(2)}, u32[]{:S(2)}) collective-permute-start(s32[]{:T(128)} %copy.90), channel_id=1, source_target_pairs={{0,4},{4,8},{8,12},{12,16},{16,20},{20,24},{24,28},{28,0},{1,5},{5... | collective-permute-start | bytes 20 | tf_op jit(solution)/shard_map/while/body/eval_jaxpr/ppermute | solution.py:18
  42.2 20.8 %collective-permute-start = (bf16[12,256,256]{2,1,0:T(8,128)(2,1)S(1)}, bf16[12,256,256]{2,1,0:T(8,128)(2,1)S(1)}, u32[]{:S(2)}, u32[]{:S(2)}) collective-permute-start(bf16[12,256,256]{2,1,0:T(8,128)(2,1)S(1)} %copy.87), channel_id=1, source_target_pairs={{0,4},{4,8},{8,12},{12,16},{16,20},{20,24},{24,28},{28,0},{1,5},{5... | collective-permute-start | bytes 4718600 | tf_op jit(solution)/shard_map/while/body/eval_jaxpr/ppermute | solution.py:18
  48.6 4.6 %copy-start.2 = (bf16[1,12]{1,0:T(2,128)(2,1)S(1)}, bf16[1,12]{1,0:T(2,128)(2,1)}, u32[]{:S(2)}) copy-start(bf16[1,12]{1,0:T(2,128)(2,1)} %get-tuple-element.417) | copy-start | bytes 76 | tf_op jit(solution)/shard_map/while
  64.8 14.7 %collective-permute-start.2 = (s32[12]{0:T(128)}, s32[12]{0:T(128)}, u32[]{:S(2)}, u32[]{:S(2)}) collective-permute-start(s32[12]{0:T(128)} %copy.89), channel_id=1, source_target_pairs={{0,4},{4,8},{8,12},{12,16},{16,20},{20,24},{24,28},{28,0},{1,5},{5... | collective-permute-start | bytes 152 | tf_op jit(solution)/shard_map/while/body/eval_jaxpr/ppermute | solution.py:18
  65.4 14.1 %collective-permute-start.1 = (s32[12]{0:T(128)S(1)}, s32[12]{0:T(128)}, u32[]{:S(2)}, u32[]{:S(2)}) collective-permute-start(s32[12]{0:T(128)S(1)} %copy.88), channel_id=1, source_target_pairs={{0,4},{4,8},{8,12},{12,16},{16,20},{20,24},{24,28},{28,0},{1,5},{5... | collective-permute-start | bytes 152 | tf_op jit(solution)/shard_map/while/body/eval_jaxpr/ppermute | solution.py:18
  67.0 12.5 %collective-permute-start.3 = (s32[]{:T(128)}, s32[]{:T(128)}, u32[]{:S(2)}, u32[]{:S(2)}) collective-permute-start(s32[]{:T(128)} %copy.90), channel_id=1, source_target_pairs={{0,4},{4,8},{8,12},{12,16},{16,20},{20,24},{24,28},{28,0},{1,5},{5... | collective-permute-start | bytes 20 | tf_op jit(solution)/shard_map/while/body/eval_jaxpr/ppermute | solution.py:18
  68.1 20.8 %collective-permute-start = (bf16[12,256,256]{2,1,0:T(8,128)(2,1)S(1)}, bf16[12,256,256]{2,1,0:T(8,128)(2,1)S(1)}, u32[]{:S(2)}, u32[]{:S(2)}) collective-permute-start(bf16[12,256,256]{2,1,0:T(8,128)(2,1)S(1)} %copy.87), channel_id=1, source_target_pairs={{0,4},{4,8},{8,12},{12,16},{16,20},{20,24},{24,28},{28,0},{1,5},{5... | collective-permute-start | bytes 4718600 | tf_op jit(solution)/shard_map/while/body/eval_jaxpr/ppermute | solution.py:18
  72.9 4.6 %copy-start.2 = (bf16[1,12]{1,0:T(2,128)(2,1)S(1)}, bf16[1,12]{1,0:T(2,128)(2,1)}, u32[]{:S(2)}) copy-start(bf16[1,12]{1,0:T(2,128)(2,1)} %get-tuple-element.417) | copy-start | bytes 76 | tf_op jit(solution)/shard_map/while
  90.7 14.4 %collective-permute-start.2 = (s32[12]{0:T(128)}, s32[12]{0:T(128)}, u32[]{:S(2)}, u32[]{:S(2)}) collective-permute-start(s32[12]{0:T(128)} %copy.89), channel_id=1, source_target_pairs={{0,4},{4,8},{8,12},{12,16},{16,20},{20,24},{24,28},{28,0},{1,5},{5... | collective-permute-start | bytes 152 | tf_op jit(solution)/shard_map/while/body/eval_jaxpr/ppermute | solution.py:18
  91.3 13.8 %collective-permute-start.1 = (s32[12]{0:T(128)S(1)}, s32[12]{0:T(128)}, u32[]{:S(2)}, u32[]{:S(2)}) collective-permute-start(s32[12]{0:T(128)S(1)} %copy.88), channel_id=1, source_target_pairs={{0,4},{4,8},{8,12},{12,16},{16,20},{20,24},{24,28},{28,0},{1,5},{5... | collective-permute-start | bytes 152 | tf_op jit(solution)/shard_map/while/body/eval_jaxpr/ppermute | solution.py:18
  91.3 13.8 %collective-permute-start.3 = (s32[]{:T(128)}, s32[]{:T(128)}, u32[]{:S(2)}, u32[]{:S(2)}) collective-permute-start(s32[]{:T(128)} %copy.90), channel_id=1, source_target_pairs={{0,4},{4,8},{8,12},{12,16},{16,20},{20,24},{24,28},{28,0},{1,5},{5... | collective-permute-start | bytes 20 | tf_op jit(solution)/shard_map/while/body/eval_jaxpr/ppermute | solution.py:18
  92.4 20.8 %collective-permute-start = (bf16[12,256,256]{2,1,0:T(8,128)(2,1)S(1)}, bf16[12,256,256]{2,1,0:T(8,128)(2,1)S(1)}, u32[]{:S(2)}, u32[]{:S(2)}) collective-permute-start(bf16[12,256,256]{2,1,0:T(8,128)(2,1)S(1)} %copy.87), channel_id=1, source_target_pairs={{0,4},{4,8},{8,12},{12,16},{16,20},{20,24},{24,28},{28,0},{1,5},{5... | collective-permute-start | bytes 4718600 | tf_op jit(solution)/shard_map/while/body/eval_jaxpr/ppermute | solution.py:18
  98.5 4.6 %copy-start.2 = (bf16[1,12]{1,0:T(2,128)(2,1)S(1)}, bf16[1,12]{1,0:T(2,128)(2,1)}, u32[]{:S(2)}) copy-start(bf16[1,12]{1,0:T(2,128)(2,1)} %get-tuple-element.417) | copy-start | bytes 76 | tf_op jit(solution)/shard_map/while
  115.0 15.1 %collective-permute-start.2 = (s32[12]{0:T(128)}, s32[12]{0:T(128)}, u32[]{:S(2)}, u32[]{:S(2)}) collective-permute-start(s32[12]{0:T(128)} %copy.89), channel_id=1, source_target_pairs={{0,4},{4,8},{8,12},{12,16},{16,20},{20,24},{24,28},{28,0},{1,5},{5... | collective-permute-start | bytes 152 | tf_op jit(solution)/shard_map/while/body/eval_jaxpr/ppermute | solution.py:18
  115.6 14.5 %collective-permute-start.1 = (s32[12]{0:T(128)S(1)}, s32[12]{0:T(128)}, u32[]{:S(2)}, u32[]{:S(2)}) collective-permute-start(s32[12]{0:T(128)S(1)} %copy.88), channel_id=1, source_target_pairs={{0,4},{4,8},{8,12},{12,16},{16,20},{20,24},{24,28},{28,0},{1,5},{5... | collective-permute-start | bytes 152 | tf_op jit(solution)/shard_map/while/body/eval_jaxpr/ppermute | solution.py:18
  116.9 13.2 %collective-permute-start.3 = (s32[]{:T(128)}, s32[]{:T(128)}, u32[]{:S(2)}, u32[]{:S(2)}) collective-permute-start(s32[]{:T(128)} %copy.90), channel_id=1, source_target_pairs={{0,4},{4,8},{8,12},{12,16},{16,20},{20,24},{24,28},{28,0},{1,5},{5... | collective-permute-start | bytes 20 | tf_op jit(solution)/shard_map/while/body/eval_jaxpr/ppermute | solution.py:18
  118.0 20.8 %collective-permute-start = (bf16[12,256,256]{2,1,0:T(8,128)(2,1)S(1)}, bf16[12,256,256]{2,1,0:T(8,128)(2,1)S(1)}, u32[]{:S(2)}, u32[]{:S(2)}) collective-permute-start(bf16[12,256,256]{2,1,0:T(8,128)(2,1)S(1)} %copy.87), channel_id=1, source_target_pairs={{0,4},{4,8},{8,12},{12,16},{16,20},{20,24},{24,28},{28,0},{1,5},{5... | collective-permute-start | bytes 4718600 | tf_op jit(solution)/shard_map/while/body/eval_jaxpr/ppermute | solution.py:18
  123.5 4.6 %copy-start.2 = (bf16[1,12]{1,0:T(2,128)(2,1)S(1)}, bf16[1,12]{1,0:T(2,128)(2,1)}, u32[]{:S(2)}) copy-start(bf16[1,12]{1,0:T(2,128)(2,1)} %get-tuple-element.417) | copy-start | bytes 76 | tf_op jit(solution)/shard_map/while
  140.6 15.4 %collective-permute-start.2 = (s32[12]{0:T(128)}, s32[12]{0:T(128)}, u32[]{:S(2)}, u32[]{:S(2)}) collective-permute-start(s32[12]{0:T(128)} %copy.89), channel_id=1, source_target_pairs={{0,4},{4,8},{8,12},{12,16},{16,20},{20,24},{24,28},{28,0},{1,5},{5... | collective-permute-start | bytes 152 | tf_op jit(solution)/shard_map/while/body/eval_jaxpr/ppermute | solution.py:18
  141.2 14.8 %collective-permute-start.1 = (s32[12]{0:T(128)S(1)}, s32[12]{0:T(128)}, u32[]{:S(2)}, u32[]{:S(2)}) collective-permute-start(s32[12]{0:T(128)S(1)} %copy.88), channel_id=1, source_target_pairs={{0,4},{4,8},{8,12},{12,16},{16,20},{20,24},{24,28},{28,0},{1,5},{5... | collective-permute-start | bytes 152 | tf_op jit(solution)/shard_map/while/body/eval_jaxpr/ppermute | solution.py:18
  141.9 14.1 %collective-permute-start.3 = (s32[]{:T(128)}, s32[]{:T(128)}, u32[]{:S(2)}, u32[]{:S(2)}) collective-permute-start(s32[]{:T(128)} %copy.90), channel_id=1, source_target_pairs={{0,4},{4,8},{8,12},{12,16},{16,20},{20,24},{24,28},{28,0},{1,5},{5... | collective-permute-start | bytes 20 | tf_op jit(solution)/shard_map/while/body/eval_jaxpr/ppermute | solution.py:18
  143.0 20.8 %collective-permute-start = (bf16[12,256,256]{2,1,0:T(8,128)(2,1)S(1)}, bf16[12,256,256]{2,1,0:T(8,128)(2,1)S(1)}, u32[]{:S(2)}, u32[]{:S(2)}) collective-permute-start(bf16[12,256,256]{2,1,0:T(8,128)(2,1)S(1)} %copy.87), channel_id=1, source_target_pairs={{0,4},{4,8},{8,12},{12,16},{16,20},{20,24},{24,28},{28,0},{1,5},{5... | collective-permute-start | bytes 4718600 | tf_op jit(solution)/shard_map/while/body/eval_jaxpr/ppermute | solution.py:18
  149.4 4.6 %copy-start.2 = (bf16[1,12]{1,0:T(2,128)(2,1)S(1)}, bf16[1,12]{1,0:T(2,128)(2,1)}, u32[]{:S(2)}) copy-start(bf16[1,12]{1,0:T(2,128)(2,1)} %get-tuple-element.417) | copy-start | bytes 76 | tf_op jit(solution)/shard_map/while
  165.6 14.7 %collective-permute-start.2 = (s32[12]{0:T(128)}, s32[12]{0:T(128)}, u32[]{:S(2)}, u32[]{:S(2)}) collective-permute-start(s32[12]{0:T(128)} %copy.89), channel_id=1, source_target_pairs={{0,4},{4,8},{8,12},{12,16},{16,20},{20,24},{24,28},{28,0},{1,5},{5... | collective-permute-start | bytes 152 | tf_op jit(solution)/shard_map/while/body/eval_jaxpr/ppermute | solution.py:18
  166.2 14.1 %collective-permute-start.1 = (s32[12]{0:T(128)S(1)}, s32[12]{0:T(128)}, u32[]{:S(2)}, u32[]{:S(2)}) collective-permute-start(s32[12]{0:T(128)S(1)} %copy.88), channel_id=1, source_target_pairs={{0,4},{4,8},{8,12},{12,16},{16,20},{20,24},{24,28},{28,0},{1,5},{5... | collective-permute-start | bytes 152 | tf_op jit(solution)/shard_map/while/body/eval_jaxpr/ppermute | solution.py:18
  167.8 12.5 %collective-permute-start.3 = (s32[]{:T(128)}, s32[]{:T(128)}, u32[]{:S(2)}, u32[]{:S(2)}) collective-permute-start(s32[]{:T(128)} %copy.90), channel_id=1, source_target_pairs={{0,4},{4,8},{8,12},{12,16},{16,20},{20,24},{24,28},{28,0},{1,5},{5... | collective-permute-start | bytes 20 | tf_op jit(solution)/shard_map/while/body/eval_jaxpr/ppermute | solution.py:18
  168.9 20.8 %collective-permute-start = (bf16[12,256,256]{2,1,0:T(8,128)(2,1)S(1)}, bf16[12,256,256]{2,1,0:T(8,128)(2,1)S(1)}, u32[]{:S(2)}, u32[]{:S(2)}) collective-permute-start(bf16[12,256,256]{2,1,0:T(8,128)(2,1)S(1)} %copy.87), channel_id=1, source_target_pairs={{0,4},{4,8},{8,12},{12,16},{16,20},{20,24},{24,28},{28,0},{1,5},{5... | collective-permute-start | bytes 4718600 | tf_op jit(solution)/shard_map/while/body/eval_jaxpr/ppermute | solution.py:18
  173.7 4.6 %copy-start.2 = (bf16[1,12]{1,0:T(2,128)(2,1)S(1)}, bf16[1,12]{1,0:T(2,128)(2,1)}, u32[]{:S(2)}) copy-start(bf16[1,12]{1,0:T(2,128)(2,1)} %get-tuple-element.417) | copy-start | bytes 76 | tf_op jit(solution)/shard_map/while
  194.4 11.9 %all-to-all-start.1 = ((bf16[1,8,1,12]{3,2,0,1:T(2,128)(2,1)}), bf16[1,8,1,12]{3,2,0,1:T(2,128)(2,1)S(1)}, u32[]{:S(2)}, u32[]{:S(2)}) async-start(bf16[1,8,1,12]{3,2,0,1:T(2,128)(2,1)} %copy.49), calls=%async_computation.1 | async-start | bytes 8192 | tf_op jit(solution)/shard_map/all_to_all | solution.py:89
  205.3 6.2 %copy-start.3 = (f32[8]{0:T(128)S(1)}, f32[8]{0:T(128)}, u32[]{:S(2)}) copy-start(f32[8]{0:T(128)} %param.16) | copy-start | bytes 100
  205.3 6.2 %copy-start.4 = (s32[4]{0:T(128)S(1)}, s32[4]{0:T(128)}, u32[]{:S(2)}) copy-start(s32[4]{0:T(128)} %param.17) | copy-start | bytes 52
  206.4 72.9 %all-to-all-start = ((bf16[64,8,1,3072]{3,0,2,1:T(8,128)(2,1)}), bf16[64,8,1,3072]{3,0,2,1:T(8,128)(2,1)S(1)}, u32[]{:S(2)}, u32[]{:S(2)}) async-start(bf16[64,8,1,3072]{3,0,2,1:T(8,128)(2,1)} %constant_dynamic-update-slice_fusion.1), calls=%async_computation | async-start | bytes 6291456 | tf_op jit(solution)/shard_map/all_to_all | solution.py:88
  279.3 1.7 copy-start.1
where the time goes:
time: 308 us; the launch traced here: 306 us
  waiting for transfers between devices  127 us (41%)
  local copies, waits for them, and re-layouts  84.7 us (28%)
  starting transfers between devices  36.6 us (12%)
  other arithmetic  26.9 us (9%)
  matrix products  24.4 us (8%)
  loops' own time  4.93 us (2%)
    all_to_all x1, waiting for transfers between devices, shards(): lax.all_to_all(stored, 'red', split_axis=1, concat_axis=2, tiled=True)  67.4 us
    ppermute x28, waiting for transfers between devices, from_behind(): return lax.ppermute(value, axis, pairs)  59.6 us
    ppermute x28, starting transfers between devices, from_behind(): return lax.ppermute(value, axis, pairs)  26.7 us
    gather x8, local copies, waits for them, and re-layouts, slot_products(): picked = jnp.take(x_blocks, col_ids, axis=1)  22.1 us
    dot_general x8, matrix products, packed_rows(): jnp.einsum('st,tvi->vsi', collect, product, precision=lax.Precision.HIGHEST)  16 us
    while x35, local copies, waits for them, and re-layouts  13.3 us
    dynamic_update_slice x9, local copies, waits for them, and re-layouts, place(): labels = lax.dynamic_update_slice_in_dim(totals[1], numbers, where_at, 0)  11.4 us
    add x1, other arithmetic, shards(): density_out = density + column_coef[:, None] * x_next  11.1 us
  transfers between devices with their start and end apart: 30, of which 8 were waited for; matrix products, arithmetic and copies ran while one was open for 28% of the time, Pallas kernels for 0%

commit v1 on v0

v1 whole, which is shorter than its diff:
```python
import functools

import jax
import jax.numpy as jnp
from jax import lax
from jax.experimental import pallas as pl
from jax.experimental.pallas import tpu as pltpu
from jax.sharding import Mesh, PartitionSpec as P

SHARES = (4, 4, 4)
DIRECT = (False, True, False)

SMEM = pl.BlockSpec(memory_space=pltpu.SMEM)
VMEM = pl.BlockSpec(memory_space=pltpu.VMEM)
ANY = pl.BlockSpec(memory_space=pl.ANY)


def chunk_sizes(capacity):
    total = sum(SHARES)
    if capacity % total == 0:
        return [part * capacity // total for part in SHARES]
    return [capacity]


def flip_slice(value, bits):
    count = 2 * lax.axis_size("red")
    return lax.ppermute(value, ("core", "red"), [(i, i ^ bits) for i in range(count)])


def flip_chip(value, bits):
    return lax.ppermute(value, "chip", [(i, i ^ bits) for i in range(lax.axis_size("chip"))])


def spread(own, chips):
    pieces = {0: [own]}
    bits = [1 << b for b in range(chips.bit_length() - 1)]
    half = own.shape[0] // 2
    halves = {}
    for bit in bits:
        whole = flip_chip(own, bit)
        pieces[bit] = [whole]
        halves[bit] = (whole[:half], whole[half:])
    direct = [pieces[bit][0] for bit in bits]
    for distance in sorted(range(chips), key=lambda d: (bin(d).count("1"), d)):
        if distance not in pieces:
            low = distance & -distance
            high = 1 << (distance.bit_length() - 1)
            first = flip_chip(halves[distance ^ high][0], high)
            second = flip_chip(halves[distance ^ low][1], low)
            halves[distance] = (first, second)
            pieces[distance] = [first, second]
    return pieces, direct


def products_kernel(layout, chips, reds, capacity, base, size, per_red, direct, *refs):
    place, mine, other = refs[:3]
    facts = refs[3 : 3 + chips]
    tiles = refs[3 + chips : 3 + chips + len(layout)]
    rest = refs[3 + chips + len(layout) :]
    if direct:
        outs, (out, picked, sems, out_sems) = rest[: 2 * reds], rest[2 * reds :]
    else:
        out, picked, sems = rest
    rows = mine.shape[0]
    width = tiles[0].shape[-1]
    chip, core, red = place[0], place[1], place[2]

    jobs = []
    for number, (distance, offset, count) in enumerate(layout):
        for local in range(count):
            jobs.append((distance, offset + local, number, local))

    def fetch(index):
        distance, slot, _, _ = jobs[index]
        column = facts[distance][0, capacity + base + slot]
        start = pl.multiple_of(column * width, width)
        return [
            pltpu.make_async_copy(
                which.at[:, pl.ds(start, width)],
                picked.at[index, pl.ds(side * rows, rows), :],
                sems.at[index, side],
            )
            for side, which in enumerate((mine, other))
        ]

    for index in range(len(jobs)):
        for copy in fetch(index):
            copy.start()
    for index in range(len(jobs)):
        for copy in fetch(index):
            copy.wait()
    for index, (distance, slot, number, local) in enumerate(jobs):
        result = lax.dot_general(
            picked[index],
            tiles[number][local],
            (((1,), (1,)), ((), ())),
            preferred_element_type=jnp.float32,
        ).astype(out.dtype)
        target_chip = jnp.bitwise_xor(chip, distance)
        target = target_chip // per_red
        row = (target_chip % per_red) * size + slot
        if direct:
            away = jnp.bitwise_xor(target, red)
            out[away, row] = result[:rows]
            out[reds + away, row] = result[rows:]
        else:
            out[core * reds + target, row] = result[:rows]
            out[(1 - core) * reds + target, row] = result[rows:]
    if direct:
        copies = [
            pltpu.make_async_copy(out.at[away], outs[away], out_sems.at[away])
            for away in range(2 * reds)
        ]
        for copy in copies:
            copy.start()
        for copy in copies:
            copy.wait()


def products(place, mine, other, facts, pieces, chips, reds, capacity, base, size, per_red, direct):
    layout, tiles = [], []
    for distance in sorted(pieces):
        offset = 0
        for array in pieces[distance]:
            layout.append((distance, offset, array.shape[0]))
            tiles.append(array)
            offset += array.shape[0]
    rows = mine.shape[0]
    width = tiles[0].shape[-1]
    jobs = chips * size
    one = (per_red * size, rows, width)
    scratch = [
        pltpu.VMEM((jobs, 2 * rows, width), jnp.bfloat16),
        pltpu.SemaphoreType.DMA((jobs, 2)),
    ]
    if direct:
        out_shape = [jax.ShapeDtypeStruct(one, jnp.bfloat16)] * (2 * reds)
        out_specs = [ANY] * (2 * reds)
        scratch = [pltpu.VMEM((2 * reds, *one), jnp.bfloat16)] + scratch
        scratch.append(pltpu.SemaphoreType.DMA((2 * reds,)))
    else:
        out_shape = jax.ShapeDtypeStruct((2 * reds, *one), jnp.bfloat16)
        out_specs = VMEM
    return pl.pallas_call(
        functools.partial(
            products_kernel, tuple(layout), chips, reds, capacity, base, size, per_red, direct
        ),
        out_shape=out_shape,
        in_specs=[SMEM, ANY, ANY] + [SMEM] * chips + [VMEM] * len(tiles),
        out_specs=out_specs,
        scratch_shapes=scratch,
    )(place, mine, other, *[facts[d] for d in range(chips)], *tiles)


def plan_kernel(sizes, directs, groups, reds, per_red, capacity, row_blocks, meta, place, table, last):
    core, red = place[1], place[2]

    def clear(i, carry):
        last[0, i] = -1
        last[1, i] = -1
        return carry

    lax.fori_loop(0, last.shape[1], clear, 0)
    position = jnp.int32(0)
    base = 0
    bound = 0
    for number, (size, direct) in enumerate(zip(sizes, directs)):
        if any(number == group[0] for group in groups):
            opening = position
        for away in range(2 * reds):
            source_core, source_red = away // reds, away % reds
            if direct:
                source_core = jnp.bitwise_xor(core, source_core)
                source_red = jnp.bitwise_xor(red, source_red)
            table[4, bound] = position
            bound += 1
            for local in range(per_red):
                panel = 2 * (red * per_red + local) + source_core
                source = panel * reds + source_red
                live = jnp.clip(meta[source, 2 * capacity] - base, 0, size)

                def enter(slot, position, local=local, source=source, source_core=source_core, base=base, size=size, opening=opening):
                    block = (2 * local + source_core) * row_blocks + meta[source, base + slot]
                    first, latest = last[0, block], last[1, block]
                    seen = first >= opening
                    lead = jnp.where(seen, first, position)
                    table[0, position] = block
                    table[1, position] = lead
                    table[2, position] = 1
                    table[3, position] = local * size + slot
                    last[0, block] = lead
                    last[1, block] = position

                    @pl.when(seen)
                    def _():
                        table[2, latest] = 0

                    return position + 1

                position = lax.fori_loop(0, live, enter, position)
        base += size
    table[4, bound] = position


def plan(meta, place, sizes, directs, groups, reds, per_red, capacity, row_blocks):
    items = max(2 * reds * per_red * capacity, 2 * reds * len(sizes) + 1)
    return pl.pallas_call(
        functools.partial(
            plan_kernel, tuple(sizes), tuple(directs), groups, reds, per_red, capacity, row_blocks
        ),
        out_shape=jax.ShapeDtypeStruct((5, items), jnp.int32),
        in_specs=[SMEM, SMEM],
        out_specs=SMEM,
        scratch_shapes=[pltpu.SMEM((2, 2 * per_red * row_blocks), jnp.int32)],
        name="plan",
    )(meta, place)


def column_factor(coeffs, potential, columns):
    slabs = potential.shape[0]
    slab = lax.broadcasted_iota(jnp.int32, (columns, 1), 0) // (columns // slabs)
    factor = jnp.zeros((columns, 1), jnp.float32)
    for s in range(slabs):
        factor = jnp.where(slab == s, coeffs[potential[s]], factor)
    return factor


def untouched_kernel(coeffs, potential, x_prev, density, x_next, density_out):
    value = -x_prev[...]
    rows = value.shape[0]
    slab = (pl.num_programs(0) * rows) // potential.shape[0]
    first = pl.program_id(0) * rows
    x_next[...] = value
    factor = coeffs[potential[first // slab]]
    density_out[...] = density[...] + factor * value


def untouched(coeffs, potential, x_prev, density, rows=8):
    columns, local_rows = x_prev.shape
    while columns // potential.shape[0] % rows:
        rows //= 2
    wide = pl.BlockSpec((rows, local_rows), lambda i: (i, 0))
    return pl.pallas_call(
        untouched_kernel,
        grid=(columns // rows,),
        out_shape=[jax.ShapeDtypeStruct(x_prev.shape, jnp.float32)] * 2,
        in_specs=[SMEM] * 2 + [wide, wide],
        out_specs=[wide, wide],
        name="untouched",
    )(coeffs, potential, x_prev, density)


def add_kernel(bound, segments, width, parts, *refs):
    table, coeffs, potential = refs[:3]
    arrived = refs[3 : 3 + parts]
    x_next, density_out, held_x, held_d, held_a, sems, sems_a = refs[5 + parts :]
    opening, closing = table[4, bound], table[4, bound + len(segments)]

    def copies(position, back):
        start = pl.multiple_of(table[0, position] * width, width)
        index = table[1, position] - opening
        result = []
        for number, (whole, held) in enumerate(((x_next, held_x), (density_out, held_d))):
            near, far = held.at[index], whole.at[:, pl.ds(start, width)]
            source, target = (near, far) if back else (far, near)
            result.append(pltpu.make_async_copy(source, target, sems.at[index, 2 * back + number]))
        return result

    def each(body):
        for number, (part, entry) in enumerate(segments):

            def step(position, carry, part=part, entry=entry):
                local = table[3, position]
                source = arrived[part]
                source = source.at[local] if entry is None else source.at[entry, local]
                index = position - opening
                body(position, pltpu.make_async_copy(source, held_a.at[index], sems_a.at[index]))
                return carry

            lax.fori_loop(table[4, bound + number], table[4, bound + number + 1], step, 0)

    def begin(position, arrival):
        @pl.when(table[1, position] == position)
        def _():
            for copy in copies(position, 0):
                copy.start()

        arrival.start()

    each(begin)
    factor = column_factor(coeffs, potential, x_next.shape[0])

    def fold(position, arrival):
        lead = table[1, position]

        @pl.when(lead == position)
        def _():
            for copy in copies(position, 0):
                copy.wait()

        arrival.wait()
        value = 2.0 * held_a[position - opening].astype(jnp.float32)
        held_x[lead - opening] += value
        held_d[lead - opening] += factor * value

        @pl.when(table[2, position] == 1)
        def _():
            for copy in copies(position, 1):
                copy.start()

    each(fold)

    def settle(position, carry):
        @pl.when(table[2, position] == 1)
        def _():
            for copy in copies(position, 1):
                copy.wait()

        return carry

    lax.fori_loop(opening, closing, settle, 0)


def add_arrived(table, coeffs, potential, chunks, x_next, density_out, bound, width):
    columns = x_next.shape[0]
    segments, arrived, items = [], [], 0
    for chunk in chunks:
        if len(chunk) == 1:
            segments += [(len(arrived), entry) for entry in range(chunk[0].shape[0])]
        else:
            segments += [(len(arrived) + entry, None) for entry in range(len(chunk))]
        arrived += chunk
        items += sum(array.size for array in chunk) // (columns * width)
    parts = len(arrived)
    return pl.pallas_call(
        functools.partial(add_kernel, bound, tuple(segments), width, parts),
        out_shape=[jax.ShapeDtypeStruct(x_next.shape, jnp.float32)] * 2,
        in_specs=[SMEM] * 3 + [ANY] * parts + [ANY, ANY],
        out_specs=[ANY, ANY],
        scratch_shapes=[
            pltpu.VMEM((items, columns, width), jnp.float32),
            pltpu.VMEM((items, columns, width), jnp.float32),
            pltpu.VMEM((items, columns, width), jnp.bfloat16),
            pltpu.SemaphoreType.DMA((items, 4)),
            pltpu.SemaphoreType.DMA((items,)),
        ],
        input_output_aliases={3 + parts: 0, 4 + parts: 1},
    )(table, coeffs, potential, *arrived, x_next, density_out)


def after(value, other):
    return lax.optimization_barrier((value, other))[0]


def work(x_now, x_prev, density, coeffs, potential, h_tiles, tile_rows, tile_cols, tile_counts):
    chips = lax.axis_size("chip")
    reds = lax.axis_size("red")
    per_red = chips // reds
    devices = 2 * chips * reds
    capacity, width = h_tiles.shape[1], h_tiles.shape[-1]
    row_blocks = x_now.shape[1] // width // (2 * per_red)
    sizes = chunk_sizes(capacity)
    directs = DIRECT[: len(sizes)]
    groups = tuple(g for g in (tuple(range(len(sizes) - 1)), (len(sizes) - 1,)) if g)
    place = jnp.stack([lax.axis_index("chip"), lax.axis_index("core"), lax.axis_index("red")])
    own_facts = jnp.concatenate([tile_rows, tile_cols, tile_counts], axis=1)
    facts = {d: flip_chip(own_facts, d) if d else own_facts for d in range(chips)}
    other = lax.ppermute(x_now, "core", [(0, 1), (1, 0)])

    base = 0
    gate = None
    landed = []
    for number, (size, direct) in enumerate(zip(sizes, directs)):
        own = h_tiles[0, base : base + size]
        if gate is not None:
            own, gate = lax.optimization_barrier((own, gate))
        pieces, gate = spread(own, chips)
        if number == 0:
            spoken = jnp.broadcast_to(after(own_facts, gate), (devices, own_facts.shape[1]))
            meta = lax.all_to_all(
                spoken, ("chip", "core", "red"), split_axis=0, concat_axis=0, tiled=True
            )
            table = plan(meta, place, sizes, directs, groups, reds, per_red, capacity, row_blocks)
        result = products(
            place, x_now, other, facts, pieces, chips, reds, capacity, base, size, per_red, direct
        )
        if direct:
            blocks = [result[0]]
            for away in range(1, 2 * reds):
                blocks.append(flip_slice(result[away], away))
            landed.append(blocks)
        else:
            landed.append(
                [lax.all_to_all(result, ("core", "red"), split_axis=0, concat_axis=0, tiled=True)]
            )
        base += size
    x_next, density_out = untouched(coeffs, potential, x_prev, density)
    for group in groups:
        x_next, density_out = add_arrived(
            table,
            coeffs,
            potential,
            [landed[chunk] for chunk in group],
            x_next,
            density_out,
            2 * reds * group[0],
            width,
        )
    return x_next, density_out


def solution(mesh):
    blk, red = mesh.shape["blk"], mesh.shape["red"]
    chips = blk // 2
    split = Mesh(mesh.devices.reshape(chips, 2, red), ("chip", "core", "red"))
    rows = ("chip", "core")
    both = P(rows, "red")
    in_specs = (both, both, both, P(), P(rows), P(rows, "red", None, None), both, both, both)
    return jax.shard_map(
        work, mesh=split, in_specs=in_specs, out_specs=(both, both), check_vma=False
    )
```

time: 308 us -> 164 us (0.53)
  local copies, waits for them, and re-layouts: 84.7 us -> 6.37 us
  waiting for transfers between devices: 127 us -> 68.2 us
  Pallas kernels: 0 us -> 45 us
  other arithmetic: 26.9 us -> 1.4 us
  matrix products: 24.4 us -> 0 us
  loops' own time: 4.93 us -> 0 us
  starting transfers between devices: 36.6 us -> 40.6 us
    all_to_all x2 -> x3, waiting for transfers between devices: 67.4 us -> 0.01 us  [the longest x2 0.01 us: work(): lax.all_to_all(result, ('core', 'red'), split_axis=0, concat_axis=0, tile...]
    pallas_call x0 -> x7, Pallas kernels: none -> 45 us  [the longest x3 14.5 us: products(): pl.pallas_call(functools.partial(products_kernel, tuple(layout), chips, r...]
    dot_general x17 -> x0, matrix products: 24.4 us -> none  [the longest x8 16 us: packed_rows(): jnp.einsum('st,tvi->vsi', collect, product, precision=lax.Precision.HIGHEST)]
    gather x8 -> x0, local copies, waits for them, and re-layouts: 22.1 us -> none  [slot_products(): picked = jnp.take(x_blocks, col_ids, axis=1)]
    dynamic_update_slice x17 -> x0, local copies, waits for them, and re-layouts: 17.6 us -> none  [the longest x9 11.4 us: place(): labels = lax.dynamic_update_slice_in_dim(totals[1], numbers, where_at, 0)]
    while x35 -> x0, local copies, waits for them, and re-layouts: 13.3 us -> none
    add x1 -> x0, other arithmetic: 11.1 us -> none  [shards(): density_out = density + column_coef[:, None] * x_next]
    convert_element_type x8 -> x0, local copies, waits for them, and re-layouts: 9.52 us -> none  [packed_rows(): summed.reshape(columns, 1, capacity * tile_width).astype(jnp.bfloat16)]
  transfers between devices with their start and end apart: 30 -> 26, of which waited for: 8 -> 11; matrix products, arithmetic and copies ran while one was open for 28% -> 3% of each run, Pallas kernels for 0% -> 25%
where the time goes in v1:
time: 164 us; the launch traced here: 163 us
  waiting for transfers between devices  68.2 us (42%)
  Pallas kernels  45 us (27%)
  starting transfers between devices  40.6 us (25%)
  local copies, waits for them, and re-layouts  6.37 us (4%)
  between operations  1.65 us (1%)
    ppermute x15, waiting for transfers between devices, flip_chip(): lax.ppermute(value, 'chip', [(i, i ^ bits) for i in range(lax.axis_size('...  49.3 us
    ppermute x15, starting transfers between devices, flip_chip(): lax.ppermute(value, 'chip', [(i, i ^ bits) for i in range(lax.axis_size('...  20.3 us
    ppermute x7, waiting for transfers between devices, flip_slice(): lax.ppermute(value, ('core', 'red'), [(i, i ^ bits) for i in range(count)])  18.8 us
    pallas_call x3, Pallas kernels, products(): pl.pallas_call(functools.partial(products_kernel, tuple(layout), chips, r...  14.5 us
    pallas_call x1, Pallas kernels, untouched(): pl.pallas_call(untouched_kernel, grid=(columns // rows,), out_shape=[jax....  13.5 us
    pallas_call x2, Pallas kernels, add_arrived(): pl.pallas_call(functools.partial(add_kernel, bound, tuple(segments), widt...  13.2 us
    all_to_all x2, starting transfers between devices, work(): lax.all_to_all(result, ('core', 'red'), split_axis=0, concat_axis=0, tile...  9.1 us
    ppermute x7, starting transfers between devices, flip_slice(): lax.ppermute(value, ('core', 'red'), [(i, i ^ bits) for i in range(count)])  5.68 us
  transfers between devices with their start and end apart: 26, of which 11 were waited for; matrix products, arithmetic and copies ran while one was open for 3% of the time, Pallas kernels for 25%

profile of v1, /device:TPU:0, one launch (start us, length us, event | category | flops | bytes accessed | tf_op | source)
XLA Modules:
  0.0 163.2 jit_solution(5793663970439750041)
XLA Ops:
  0.6 0.6 collective-permute-start.2
  1.2 1.5 slice_bitcast_fusion
  2.7 2.6 %collective-permute-start.1 = (bf16[4,256,256]{2,1,0:T(8,128)(2,1)S(1)}, bf16[4,256,256]{2,1,0:T(8,128)(2,1)S(1)}, u32[]{:S(2)}, u32[]{:S(2)}) collective-permute-start(bf16[4,256,256]{2,1,0:T(8,128)(2,1)S(1)} %get-tuple-element.33.refs_7_), channel_id=1, source_target_pairs={{0,16},{8,24},{16,0},{24,8},{1,17},{9,25},{17,1},{25,9},{2,18},{10... | collective-permute-start | bytes 1572872 | tf_op jit(solution)/shard_map/ppermute | solution.py:31
  5.3 1.5 collective-permute-start
  6.8 11.1 %collective-permute-done.1.refs_9_ = bf16[4,256,256]{2,1,0:T(8,128)(2,1)S(1)} collective-permute-done((bf16[4,256,256]{2,1,0:T(8,128)(2,1)S(1)}, bf16[4,256,256]{2,1,0:T(8,128)(2,1)S(1)}, u32[]{:S(2)}, u32[]{:S(2)}) %collective-permute-start.1) | collective-permute-done | bytes 524320 | tf_op jit(solution)/shard_map/ppermute | solution.py:31
  17.9 1.8 %collective-permute-start.13 = (bf16[2,256,256]{2,1,0:T(8,128)(2,1)S(1)}, bf16[2,256,256]{2,1,0:T(8,128)(2,1)S(1)}, u32[]{:S(2)}, u32[]{:S(2)}) collective-permute-start(bf16[2,256,256]{2,1,0:T(8,128)(2,1)S(1)} %slice.39), channel_id=1, source_target_pairs={{0,8},{8,0},{16,24},{24,16},{1,9},{9,1},{17,25},{25,17},{2,10},{10... | collective-permute-start | bytes 786440 | tf_op jit(solution)/shard_map/ppermute | solution.py:31
  19.7 0.8 slice.38
  20.4 1.5 collective-permute-start.12
  22.6 0.7 pad_add_fusion.refs_3_
  23.4 1.1 collective-permute-start.5
  24.5 0.9 collective-permute-start.4
  25.4 0.6 broadcast_in_dim.2
  26.0 4.9 %all-to-all-start = ((s32[32,1,25]{2,1,0:T(1,128)}), s32[32,1,25]{2,1,0:T(1,128)S(1)}, u32[]{:S(2)}, u32[]{:S(2)}) async-start(s32[32,1,25]{2,1,0:T(1,128)} %broadcast_in_dim.2), calls=%async_computation | async-start | bytes 32768 | tf_op jit(solution)/shard_map/all_to_all | solution.py:380
  30.9 1.8 %collective-permute-start.3 = (s32[1,25]{1,0:T(1,128)S(1)}, s32[1,25]{1,0:T(1,128)S(1)}, u32[]{:S(2)}, u32[]{:S(2)}) collective-permute-start(s32[1,25]{1,0:T(1,128)S(1)} %pad_add_fusion.refs_3_), channel_id=1, source_target_pairs={{0,8},{8,0},{16,24},{24,16},{1,9},{9,1},{17,25},{25,17},{2,10},{10... | collective-permute-start | bytes 308 | tf_op jit(solution)/shard_map/ppermute | solution.py:31
  32.7 0.7 pad_add_fusion.1.place.refs_0_
  33.4 1.1 collective-permute-done.3.refs_4_
  35.4 4.8 %shard_map.105 = bf16[8,4,64,256]{3,2,1,0:T(8,128)(2,1)} custom-call(s32[3]{0:T(128)} %pad_add_fusion.1.place.refs_0_, bf16[64,32768]{1,0:T(8,128)(2,1)} %refs_1_.7, bf16[64,32768]{1,0:T(8,128)(2,1)} %collective-permute-done.2.refs_2_, s32[1,25]{1,0:T(1,128)} %copy-done.23, s32[1,25]{1,0:T(1,128)} %copy-done.26, s32[1,25]{1,0:T(1,128)} %copy-done.25, ...), custom_call_target="tpu_custom_call" | custom-call | tf_op jit(solution)/shard_map/pallas_call | solution.py:144
  40.2 4.9 %all-to-all-start.2 = ((bf16[8,4,64,256]{3,2,1,0:T(8,128)(2,1)}), bf16[8,4,64,256]{3,2,1,0:T(8,128)(2,1)S(1)}, u32[]{:S(2)}, u32[]{:S(2)}) async-start(bf16[8,4,64,256]{3,2,1,0:T(8,128)(2,1)} %shard_map.105), calls=%async_computation.2 | async-start | bytes 2097152 | tf_op jit(solution)/shard_map/all_to_all | solution.py:394
  45.1 1.5 collective-permute-start.7
  46.6 1.5 collective-permute-start.6
  48.0 11.4 %collective-permute-done.7.refs_9_ = bf16[4,256,256]{2,1,0:T(8,128)(2,1)S(1)} collective-permute-done((bf16[4,256,256]{2,1,0:T(8,128)(2,1)S(1)}, bf16[4,256,256]{2,1,0:T(8,128)(2,1)S(1)}, u32[]{:S(2)}, u32[]{:S(2)}) %collective-permute-start.7) | collective-permute-done | bytes 524320 | tf_op jit(solution)/shard_map/ppermute | solution.py:31
  59.4 1.2 collective-permute-done.6.refs_8_
  60.6 0.5 collective-permute-start.9
  61.1 1.5 collective-permute-start.8
  62.6 11.2 %collective-permute-done.9.refs_9_ = bf16[4,256,256]{2,1,0:T(8,128)(2,1)S(1)} collective-permute-done((bf16[4,256,256]{2,1,0:T(8,128)(2,1)S(1)}, bf16[4,256,256]{2,1,0:T(8,128)(2,1)S(1)}, u32[]{:S(2)}, u32[]{:S(2)}) %collective-permute-start.9) | collective-permute-done | bytes 524320 | tf_op jit(solution)/shard_map/ppermute | solution.py:31
  73.8 1.5 collective-permute-start.11
  75.4 0.8 copy-done.10
  76.2 0.6 collective-permute-start.10
  76.8 3.8 %collective-permute-done.11.refs_11_ = bf16[2,256,256]{2,1,0:T(8,128)(2,1)S(1)} collective-permute-done((bf16[2,256,256]{2,1,0:T(8,128)(2,1)S(1)}, bf16[2,256,256]{2,1,0:T(8,128)(2,1)S(1)}, u32[]{:S(2)}, u32[]{:S(2)}) %collective-permute-start.11) | collective-permute-done | bytes 262176 | tf_op jit(solution)/shard_map/ppermute | solution.py:31
  80.6 2.1 %collective-permute-done.10.refs_10_ = bf16[2,256,256]{2,1,0:T(8,128)(2,1)} collective-permute-done((bf16[2,256,256]{2,1,0:T(8,128)(2,1)S(1)}, bf16[2,256,256]{2,1,0:T(8,128)(2,1)}, u32[]{:S(2)}, u32[]{:S(2)}) %collective-permute-start.10) | collective-permute-done | bytes 262176 | tf_op jit(solution)/shard_map/ppermute | solution.py:31
  82.7 4.9 %shard_map.104 = bf16[8,4,64,256]{3,2,1,0:T(8,128)(2,1)} custom-call(s32[3]{0:T(128)} %pad_add_fusion.1.place.refs_0_, bf16[64,32768]{1,0:T(8,128)(2,1)} %refs_1_.7, bf16[64,32768]{1,0:T(8,128)(2,1)} %collective-permute-done.2.refs_2_, s32[1,25]{1,0:T(1,128)} %copy-done.23, s32[1,25]{1,0:T(1,128)} %copy-done.26, s32[1,25]{1,0:T(1,128)} %copy-done.25, ...), custom_call_target="tpu_custom_call" | custom-call | tf_op jit(solution)/shard_map/pallas_call | solution.py:144
  87.7 4.2 %all-to-all-start.1 = ((bf16[8,4,64,256]{3,2,1,0:T(8,128)(2,1)}), bf16[8,4,64,256]{3,2,1,0:T(8,128)(2,1)S(1)}, u32[]{:S(2)}, u32[]{:S(2)}) async-start(bf16[8,4,64,256]{3,2,1,0:T(8,128)(2,1)} %shard_map.104), calls=%async_computation.1 | async-start | bytes 2097152 | tf_op jit(solution)/shard_map/all_to_all | solution.py:394
  91.9 0.8 collective-permute-start.15
  92.7 1.2 collective-permute-start.14
  93.9 6.8 %collective-permute-done.15.refs_11_ = bf16[2,256,256]{2,1,0:T(8,128)(2,1)S(1)} collective-permute-done((bf16[2,256,256]{2,1,0:T(8,128)(2,1)S(1)}, bf16[2,256,256]{2,1,0:T(8,128)(2,1)S(1)}, u32[]{:S(2)}, u32[]{:S(2)}) %collective-permute-start.15) | collective-permute-done | bytes 262176 | tf_op jit(solution)/shard_map/ppermute | solution.py:31
  100.7 0.6 collective-permute-done.14.refs_10_
  101.4 4.8 %shard_map.106 = (bf16[4,64,256]{2,1,0:T(8,128)(2,1)}, bf16[4,64,256]{2,1,0:T(8,128)(2,1)}, bf16[4,64,256]{2,1,0:T(8,128)(2,1)}, bf16[4,64,256]{2,1,0:T(8,128)(2...) custom-call(s32[3]{0:T(128)} %pad_add_fusion.1.place.refs_0_, ...), custom_call_target="tpu_custom_call" | custom-call | tf_op jit(solution)/shard_map/pallas_call | solution.py:144
  106.2 1.7 %collective-permute-start.16 = (bf16[4,64,256]{2,1,0:T(8,128)(2,1)}, bf16[4,64,256]{2,1,0:T(8,128)(2,1)S(1)}, u32[]{:S(2)}, u32[]{:S(2)}) collective-permute-start(bf16[4,64,256]{2,1,0:T(8,128)(2,1)} %get-tuple-element.21), channel_id=1, source_target_pairs={{0,1},{1,0},{2,3},{3,2},{4,5},{5,4},{6,7},{7,6},{8,9},{9,8},{10,11... | collective-permute-start | bytes 393224 | tf_op jit(solution)/shard_map/ppermute | solution.py:27
  107.9 2.4 %collective-permute-start.17 = (bf16[4,64,256]{2,1,0:T(8,128)(2,1)}, bf16[4,64,256]{2,1,0:T(8,128)(2,1)S(1)}, u32[]{:S(2)}, u32[]{:S(2)}) collective-permute-start(bf16[4,64,256]{2,1,0:T(8,128)(2,1)} %get-tuple-element.22), channel_id=1, source_target_pairs={{0,2},{1,3},{2,0},{3,1},{4,6},{5,7},{6,4},{7,5},{8,10},{9,11},{10,... | collective-permute-start | bytes 393224 | tf_op jit(solution)/shard_map/ppermute | solution.py:27
  110.7 0.8 collective-permute-start.20
  111.5 8.6 %collective-permute-done.16.refs_5_ = bf16[4,64,256]{2,1,0:T(8,128)(2,1)S(1)} collective-permute-done((bf16[4,64,256]{2,1,0:T(8,128)(2,1)}, bf16[4,64,256]{2,1,0:T(8,128)(2,1)S(1)}, u32[]{:S(2)}, u32[]{:S(2)}) %collective-permute-start.16) | collective-permute-done | bytes 131104 | tf_op jit(solution)/shard_map/ppermute | solution.py:27
  120.1 10.2 %collective-permute-done.17.refs_6_ = bf16[4,64,256]{2,1,0:T(8,128)(2,1)S(1)} collective-permute-done((bf16[4,64,256]{2,1,0:T(8,128)(2,1)}, bf16[4,64,256]{2,1,0:T(8,128)(2,1)S(1)}, u32[]{:S(2)}, u32[]{:S(2)}) %collective-permute-start.17) | collective-permute-done | bytes 131104 | tf_op jit(solution)/shard_map/ppermute | solution.py:27
  130.7 13.5 %untouched.1 = (f32[64,32768]{1,0:T(8,128)}, f32[64,32768]{1,0:T(8,128)}) custom-call(f32[8]{0:T(128)} %refs_1_.9, s32[4]{0:T(128)} %refs_2_.3, f32[64,32768]{1,0:T(8,128)} %x_prev.1, f32[64,32768]{1,0:T(8,128)} %density.1), custom_call_target="tpu_custom_call" | custom-call | tf_op jit(solution)/shard_map/untouched/pallas_call | solution.py:243
  144.3 3.8 %plan.1.refs_0_ = s32[5,96]{1,0:T(8,128)} custom-call(s32[32,25]{1,0:T(8,128)} %bitcast.11, s32[3]{0:T(128)} %pad_add_fusion.1.place.refs_0_), custom_call_target="tpu_custom_call" | custom-call | tf_op jit(solution)/shard_map/plan/pallas_call | solution.py:207
  148.1 0.6 copy-done.17
  148.9 9.0 %shard_map.107 = (f32[64,32768]{1,0:T(8,128)}, f32[64,32768]{1,0:T(8,128)}) custom-call(s32[5,96]{1,0:T(8,128)} %plan.1.refs_0_, f32[8]{0:T(128)} %refs_1_.9, s32[4]{0:T(128)} %refs_2_.3, bf16[8,4,64,256]{3,2,1,0:T(8,128)(2,1)} %copy-done.1, bf16[4,64,256]{2,1,0:T(8,128)(2,1)} %get-tuple-element.20.refs_4_, ...), custom_call_target="tpu_custom_call", output_to_operand_aliasing={{0}: (12, {}), {1}: (13, {})} | custom-call | tf_op jit(solution)/shard_map/pallas_call | solution.py:335
  157.9 1.0 copy-done
  158.9 4.3 %shard_map.108 = (f32[64,32768]{1,0:T(8,128)}, f32[64,32768]{1,0:T(8,128)}) custom-call(s32[5,96]{1,0:T(8,128)} %plan.1.refs_0_, f32[8]{0:T(128)} %refs_1_.9, s32[4]{0:T(128)} %refs_2_.3, bf16[8,4,64,256]{3,2,1,0:T(8,128)(2,1)} %copy-done, f32[64,32768]{1,0:T(8,128)} %get-tuple-element.30.refs_4_, ...), custom_call_target="tpu_custom_call", output_to_operand_aliasing={{0}: (4, {}), {1}: (5, {})} | custom-call | tf_op jit(solution)/shard_map/pallas_call | solution.py:335
  (75 shorter events, 2.0 us)
Async XLA Ops:
  0.6 33.9 %collective-permute-start.2 = (bf16[64,32768]{1,0:T(8,128)(2,1)}, bf16[64,32768]{1,0:T(8,128)(2,1)}, u32[]{:S(2)}, u32[]{:S(2)}) collective-permute-start(bf16[64,32768]{1,0:T(8,128)(2,1)} %refs_1_.7), channel_id=1, source_target_pairs={{0,4},{4,0},{1,5},{5,1},{2,6},{6,2},{3,7},{7,3},{8,12},{12,8},{9,1... | collective-permute-start | bytes 12582920 | tf_op jit(solution)/shard_map/ppermute | solution.py:368
  2.6 31.9 %copy-start.4 = (bf16[4,256,256]{2,1,0:T(8,128)(2,1)}, bf16[4,256,256]{2,1,0:T(8,128)(2,1)S(1)}, u32[]{:S(2)}) copy-start(bf16[4,256,256]{2,1,0:T(8,128)(2,1)S(1)} %get-tuple-element.33.refs_7_) | copy-start | bytes 1572868
  2.7 80.1 %copy-start.3 = (bf16[4,256,256]{2,1,0:T(8,128)(2,1)}, bf16[4,256,256]{2,1,0:T(8,128)(2,1)S(1)}, u32[]{:S(2)}) copy-start(bf16[4,256,256]{2,1,0:T(8,128)(2,1)S(1)} %get-tuple-element.19.refs_7_) | copy-start | bytes 1572868
  2.7 85.0 %copy-start.2 = (bf16[4,256,256]{2,1,0:T(8,128)(2,1)}, bf16[4,256,256]{2,1,0:T(8,128)(2,1)S(1)}, u32[]{:S(2)}) copy-start(bf16[4,256,256]{2,1,0:T(8,128)(2,1)S(1)} %get-tuple-element.18.refs_7_) | copy-start | bytes 1572868
  2.7 15.2 %collective-permute-start.1 = (bf16[4,256,256]{2,1,0:T(8,128)(2,1)S(1)}, bf16[4,256,256]{2,1,0:T(8,128)(2,1)S(1)}, u32[]{:S(2)}, u32[]{:S(2)}) collective-permute-start(bf16[4,256,256]{2,1,0:T(8,128)(2,1)S(1)} %get-tuple-element.33.refs_7_), channel_id=1, source_target_pairs={{0,16},{8,24},{16,0},{24,8},{1,17},{9,25},{17,1},{25,9},{2,18},{10... | collective-permute-start | bytes 1572872 | tf_op jit(solution)/shard_map/ppermute | solution.py:31
  5.3 14.4 %collective-permute-start = (bf16[4,256,256]{2,1,0:T(8,128)(2,1)S(1)}, bf16[4,256,256]{2,1,0:T(8,128)(2,1)S(1)}, u32[]{:S(2)}, u32[]{:S(2)}) collective-permute-start(bf16[4,256,256]{2,1,0:T(8,128)(2,1)S(1)} %get-tuple-element.33.refs_7_), channel_id=1, source_target_pairs={{0,8},{8,0},{16,24},{24,16},{1,9},{9,1},{17,25},{25,17},{2,10},{10... | collective-permute-start | bytes 1572872 | tf_op jit(solution)/shard_map/ppermute | solution.py:31
  17.8 16.7 %copy-start.7 = (bf16[4,256,256]{2,1,0:T(8,128)(2,1)}, bf16[4,256,256]{2,1,0:T(8,128)(2,1)S(1)}, u32[]{:S(2)}) copy-start(bf16[4,256,256]{2,1,0:T(8,128)(2,1)S(1)} %collective-permute-done.1.refs_9_) | copy-start | bytes 1572868
  17.9 16.7 %collective-permute-start.13 = (bf16[2,256,256]{2,1,0:T(8,128)(2,1)S(1)}, bf16[2,256,256]{2,1,0:T(8,128)(2,1)S(1)}, u32[]{:S(2)}, u32[]{:S(2)}) collective-permute-start(bf16[2,256,256]{2,1,0:T(8,128)(2,1)S(1)} %slice.39), channel_id=1, source_target_pairs={{0,8},{8,0},{16,24},{24,16},{1,9},{9,1},{17,25},{25,17},{2,10},{10... | collective-permute-start | bytes 786440 | tf_op jit(solution)/shard_map/ppermute | solution.py:31
  19.7 14.9 %copy-start.8 = (bf16[4,256,256]{2,1,0:T(8,128)(2,1)}, bf16[4,256,256]{2,1,0:T(8,128)(2,1)S(1)}, u32[]{:S(2)}) copy-start(bf16[4,256,256]{2,1,0:T(8,128)(2,1)S(1)} %collective-permute-done.refs_8_) | copy-start | bytes 1572868
  20.4 14.1 %collective-permute-start.12 = (bf16[2,256,256]{2,1,0:T(8,128)(2,1)}, bf16[2,256,256]{2,1,0:T(8,128)(2,1)S(1)}, u32[]{:S(2)}, u32[]{:S(2)}) collective-permute-start(bf16[2,256,256]{2,1,0:T(8,128)(2,1)} %slice.38), channel_id=1, source_target_pairs={{0,16},{8,24},{16,0},{24,8},{1,17},{9,25},{17,1},{25,9},{2,18},{10... | collective-permute-start | bytes 786440 | tf_op jit(solution)/shard_map/ppermute | solution.py:31
  23.4 11.2 %copy-start.23 = (s32[1,25]{1,0:T(1,128)}, s32[1,25]{1,0:T(1,128)S(1)}, u32[]{:S(2)}) copy-start(s32[1,25]{1,0:T(1,128)S(1)} %pad_add_fusion.refs_3_) | copy-start | bytes 304
  23.4 7.5 %collective-permute-start.5 = (s32[1,25]{1,0:T(1,128)S(1)}, s32[1,25]{1,0:T(1,128)S(1)}, u32[]{:S(2)}, u32[]{:S(2)}) collective-permute-start(s32[1,25]{1,0:T(1,128)S(1)} %pad_add_fusion.refs_3_), channel_id=1, source_target_pairs={{0,24},{8,16},{16,8},{24,0},{1,25},{9,17},{17,9},{25,1},{2,26},{10... | collective-permute-start | bytes 308 | tf_op jit(solution)/shard_map/ppermute | solution.py:31
  24.5 8.9 %collective-permute-start.4 = (s32[1,25]{1,0:T(1,128)S(1)}, s32[1,25]{1,0:T(1,128)S(1)}, u32[]{:S(2)}, u32[]{:S(2)}) collective-permute-start(s32[1,25]{1,0:T(1,128)S(1)} %pad_add_fusion.refs_3_), channel_id=1, source_target_pairs={{0,16},{8,24},{16,0},{24,8},{1,17},{9,25},{17,1},{25,9},{2,18},{10... | collective-permute-start | bytes 308 | tf_op jit(solution)/shard_map/ppermute | solution.py:31
  26.0 14.2 %all-to-all-start = ((s32[32,1,25]{2,1,0:T(1,128)}), s32[32,1,25]{2,1,0:T(1,128)S(1)}, u32[]{:S(2)}, u32[]{:S(2)}) async-start(s32[32,1,25]{2,1,0:T(1,128)} %broadcast_in_dim.2), calls=%async_computation | async-start | bytes 32768 | tf_op jit(solution)/shard_map/all_to_all | solution.py:380
  30.9 3.7 %copy-start.24 = (s32[1,25]{1,0:T(1,128)}, s32[1,25]{1,0:T(1,128)S(1)}, u32[]{:S(2)}) copy-start(s32[1,25]{1,0:T(1,128)S(1)} %collective-permute-done.5.refs_6_) | copy-start | bytes 304
  30.9 3.6 %collective-permute-start.3 = (s32[1,25]{1,0:T(1,128)S(1)}, s32[1,25]{1,0:T(1,128)S(1)}, u32[]{:S(2)}, u32[]{:S(2)}) collective-permute-start(s32[1,25]{1,0:T(1,128)S(1)} %pad_add_fusion.refs_3_), channel_id=1, source_target_pairs={{0,8},{8,0},{16,24},{24,16},{1,9},{9,1},{17,25},{25,17},{2,10},{10... | collective-permute-start | bytes 308 | tf_op jit(solution)/shard_map/ppermute | solution.py:31
  33.4 1.2 copy-start.25
  34.5 0.7 copy-start.11
  34.5 0.8 copy-start.12
  40.1 47.5 %copy-start.22 = (s32[32,1,25]{2,1,0:T(1,128)}, s32[32,1,25]{2,1,0:T(1,128)S(1)}, u32[]{:S(2)}) copy-start(s32[32,1,25]{2,1,0:T(1,128)S(1)} %all-to-all-done) | copy-start | bytes 9604
  40.2 47.5 %all-to-all-start.2 = ((bf16[8,4,64,256]{3,2,1,0:T(8,128)(2,1)}), bf16[8,4,64,256]{3,2,1,0:T(8,128)(2,1)S(1)}, u32[]{:S(2)}, u32[]{:S(2)}) async-start(bf16[8,4,64,256]{3,2,1,0:T(8,128)(2,1)} %shard_map.105), calls=%async_computation.2 | async-start | bytes 2097152 | tf_op jit(solution)/shard_map/all_to_all | solution.py:394
  45.1 14.3 %collective-permute-start.7 = (bf16[4,256,256]{2,1,0:T(8,128)(2,1)S(1)}, bf16[4,256,256]{2,1,0:T(8,128)(2,1)S(1)}, u32[]{:S(2)}, u32[]{:S(2)}) collective-permute-start(bf16[4,256,256]{2,1,0:T(8,128)(2,1)S(1)} %get-tuple-element.18.refs_7_), channel_id=1, source_target_pairs={{0,16},{8,24},{16,0},{24,8},{1,17},{9,25},{17,1},{25,9},{2,18},{10... | collective-permute-start | bytes 1572872 | tf_op jit(solution)/shard_map/ppermute | solution.py:31
  46.6 14.1 %collective-permute-start.6 = (bf16[4,256,256]{2,1,0:T(8,128)(2,1)S(1)}, bf16[4,256,256]{2,1,0:T(8,128)(2,1)S(1)}, u32[]{:S(2)}, u32[]{:S(2)}) collective-permute-start(bf16[4,256,256]{2,1,0:T(8,128)(2,1)S(1)} %get-tuple-element.18.refs_7_), channel_id=1, source_target_pairs={{0,8},{8,0},{16,24},{24,16},{1,9},{9,1},{17,25},{25,17},{2,10},{10... | collective-permute-start | bytes 1572872 | tf_op jit(solution)/shard_map/ppermute | solution.py:31
  59.4 41.9 %copy-start.5 = (bf16[4,256,256]{2,1,0:T(8,128)(2,1)}, bf16[4,256,256]{2,1,0:T(8,128)(2,1)S(1)}, u32[]{:S(2)}) copy-start(bf16[4,256,256]{2,1,0:T(8,128)(2,1)S(1)} %collective-permute-done.7.refs_9_) | copy-start | bytes 1572868
  60.6 40.7 %copy-start.6 = (bf16[4,256,256]{2,1,0:T(8,128)(2,1)}, bf16[4,256,256]{2,1,0:T(8,128)(2,1)S(1)}, u32[]{:S(2)}) copy-start(bf16[4,256,256]{2,1,0:T(8,128)(2,1)S(1)} %collective-permute-done.6.refs_8_) | copy-start | bytes 1572868
  60.6 13.2 %collective-permute-start.9 = (bf16[4,256,256]{2,1,0:T(8,128)(2,1)S(1)}, bf16[4,256,256]{2,1,0:T(8,128)(2,1)S(1)}, u32[]{:S(2)}, u32[]{:S(2)}) collective-permute-start(bf16[4,256,256]{2,1,0:T(8,128)(2,1)S(1)} %get-tuple-element.19.refs_7_), channel_id=1, source_target_pairs={{0,16},{8,24},{16,0},{24,8},{1,17},{9,25},{17,1},{25,9},{2,18},{10... | collective-permute-start | bytes 1572872 | tf_op jit(solution)/shard_map/ppermute | solution.py:31
  61.1 14.2 %collective-permute-start.8 = (bf16[4,256,256]{2,1,0:T(8,128)(2,1)S(1)}, bf16[4,256,256]{2,1,0:T(8,128)(2,1)S(1)}, u32[]{:S(2)}, u32[]{:S(2)}) collective-permute-start(bf16[4,256,256]{2,1,0:T(8,128)(2,1)S(1)} %get-tuple-element.19.refs_7_), channel_id=1, source_target_pairs={{0,8},{8,0},{16,24},{24,16},{1,9},{9,1},{17,25},{25,17},{2,10},{10... | collective-permute-start | bytes 1572872 | tf_op jit(solution)/shard_map/ppermute | solution.py:31
  73.8 1.6 copy-start.9
  73.8 6.8 %collective-permute-start.11 = (bf16[2,256,256]{2,1,0:T(8,128)(2,1)S(1)}, bf16[2,256,256]{2,1,0:T(8,128)(2,1)S(1)}, u32[]{:S(2)}, u32[]{:S(2)}) collective-permute-start(bf16[2,256,256]{2,1,0:T(8,128)(2,1)S(1)} %slice.37), channel_id=1, source_target_pairs={{0,8},{8,0},{16,24},{24,16},{1,9},{9,1},{17,25},{25,17},{2,10},{10... | collective-permute-start | bytes 786440 | tf_op jit(solution)/shard_map/ppermute | solution.py:31
  75.4 0.8 copy-start.10
  76.2 6.5 %collective-permute-start.10 = (bf16[2,256,256]{2,1,0:T(8,128)(2,1)S(1)}, bf16[2,256,256]{2,1,0:T(8,128)(2,1)}, u32[]{:S(2)}, u32[]{:S(2)}) collective-permute-start(bf16[2,256,256]{2,1,0:T(8,128)(2,1)S(1)} %slice.36), channel_id=1, source_target_pairs={{0,16},{8,24},{16,0},{24,8},{1,17},{9,25},{17,1},{25,9},{2,18},{10... | collective-permute-start | bytes 786440 | tf_op jit(solution)/shard_map/ppermute | solution.py:31
  80.6 2.1 %copy-start.14 = (bf16[2,256,256]{2,1,0:T(8,128)(2,1)}, bf16[2,256,256]{2,1,0:T(8,128)(2,1)S(1)}, u32[]{:S(2)}) copy-start(bf16[2,256,256]{2,1,0:T(8,128)(2,1)S(1)} %collective-permute-done.11.refs_11_) | copy-start | bytes 786436
  87.6 56.6 %copy-start.1 = (bf16[8,4,64,256]{3,2,1,0:T(8,128)(2,1)}, bf16[8,4,64,256]{3,2,1,0:T(8,128)(2,1)S(1)}, u32[]{:S(2)}) copy-start(bf16[8,4,64,256]{3,2,1,0:T(8,128)(2,1)S(1)} %all-to-all-done.2.refs_3_) | copy-start | bytes 3145732
  87.7 70.2 %all-to-all-start.1 = ((bf16[8,4,64,256]{3,2,1,0:T(8,128)(2,1)}), bf16[8,4,64,256]{3,2,1,0:T(8,128)(2,1)S(1)}, u32[]{:S(2)}, u32[]{:S(2)}) async-start(bf16[8,4,64,256]{3,2,1,0:T(8,128)(2,1)} %shard_map.104), calls=%async_computation.1 | async-start | bytes 2097152 | tf_op jit(solution)/shard_map/all_to_all | solution.py:394
  91.9 8.8 %collective-permute-start.15 = (bf16[2,256,256]{2,1,0:T(8,128)(2,1)S(1)}, bf16[2,256,256]{2,1,0:T(8,128)(2,1)S(1)}, u32[]{:S(2)}, u32[]{:S(2)}) collective-permute-start(bf16[2,256,256]{2,1,0:T(8,128)(2,1)S(1)} %slice.41), channel_id=1, source_target_pairs={{0,8},{8,0},{16,24},{24,16},{1,9},{9,1},{17,25},{25,17},{2,10},{10... | collective-permute-start | bytes 786440 | tf_op jit(solution)/shard_map/ppermute | solution.py:31
  92.7 8.6 %collective-permute-start.14 = (bf16[2,256,256]{2,1,0:T(8,128)(2,1)S(1)}, bf16[2,256,256]{2,1,0:T(8,128)(2,1)}, u32[]{:S(2)}, u32[]{:S(2)}) collective-permute-start(bf16[2,256,256]{2,1,0:T(8,128)(2,1)S(1)} %slice.40), channel_id=1, source_target_pairs={{0,16},{8,24},{16,0},{24,8},{1,17},{9,25},{17,1},{25,9},{2,18},{10... | collective-permute-start | bytes 786440 | tf_op jit(solution)/shard_map/ppermute | solution.py:31
  106.2 13.9 %collective-permute-start.16 = (bf16[4,64,256]{2,1,0:T(8,128)(2,1)}, bf16[4,64,256]{2,1,0:T(8,128)(2,1)S(1)}, u32[]{:S(2)}, u32[]{:S(2)}) collective-permute-start(bf16[4,64,256]{2,1,0:T(8,128)(2,1)} %get-tuple-element.21), channel_id=1, source_target_pairs={{0,1},{1,0},{2,3},{3,2},{4,5},{5,4},{6,7},{7,6},{8,9},{9,8},{10,11... | collective-permute-start | bytes 393224 | tf_op jit(solution)/shard_map/ppermute | solution.py:27
  107.9 22.4 %collective-permute-start.17 = (bf16[4,64,256]{2,1,0:T(8,128)(2,1)}, bf16[4,64,256]{2,1,0:T(8,128)(2,1)S(1)}, u32[]{:S(2)}, u32[]{:S(2)}) collective-permute-start(bf16[4,64,256]{2,1,0:T(8,128)(2,1)} %get-tuple-element.22), channel_id=1, source_target_pairs={{0,2},{1,3},{2,0},{3,1},{4,6},{5,7},{6,4},{7,5},{8,10},{9,11},{10,... | collective-permute-start | bytes 393224 | tf_op jit(solution)/shard_map/ppermute | solution.py:27
  110.2 37.8 %collective-permute-start.18 = (bf16[4,64,256]{2,1,0:T(8,128)(2,1)}, bf16[4,64,256]{2,1,0:T(8,128)(2,1)S(1)}, u32[]{:S(2)}, u32[]{:S(2)}) collective-permute-start(bf16[4,64,256]{2,1,0:T(8,128)(2,1)} %get-tuple-element.23), channel_id=1, source_target_pairs={{0,3},{1,2},{2,1},{3,0},{4,7},{5,6},{6,5},{7,4},{8,11},{9,10},{10,... | collective-permute-start | bytes 393224 | tf_op jit(solution)/shard_map/ppermute | solution.py:27
  110.7 37.4 %collective-permute-start.19 = (bf16[4,64,256]{2,1,0:T(8,128)(2,1)}, bf16[4,64,256]{2,1,0:T(8,128)(2,1)S(1)}, u32[]{:S(2)}, u32[]{:S(2)}) collective-permute-start(bf16[4,64,256]{2,1,0:T(8,128)(2,1)} %get-tuple-element.24), channel_id=1, source_target_pairs={{0,4},{1,5},{2,6},{3,7},{4,0},{5,1},{6,2},{7,3},{8,12},{9,13},{10,... | collective-permute-start | bytes 393224 | tf_op jit(solution)/shard_map/ppermute | solution.py:27
  110.7 37.4 %collective-permute-start.20 = (bf16[4,64,256]{2,1,0:T(8,128)(2,1)}, bf16[4,64,256]{2,1,0:T(8,128)(2,1)S(1)}, u32[]{:S(2)}, u32[]{:S(2)}) collective-permute-start(bf16[4,64,256]{2,1,0:T(8,128)(2,1)} %get-tuple-element.25), channel_id=1, source_target_pairs={{0,5},{1,4},{2,7},{3,6},{4,1},{5,0},{6,3},{7,2},{8,13},{9,12},{10,... | collective-permute-start | bytes 393224 | tf_op jit(solution)/shard_map/ppermute | solution.py:27
  120.1 24.1 %copy-start.15 = (bf16[4,64,256]{2,1,0:T(8,128)(2,1)}, bf16[4,64,256]{2,1,0:T(8,128)(2,1)S(1)}, u32[]{:S(2)}) copy-start(bf16[4,64,256]{2,1,0:T(8,128)(2,1)S(1)} %collective-permute-done.16.refs_5_) | copy-start | bytes 393220
  120.1 28.0 %collective-permute-start.21 = (bf16[4,64,256]{2,1,0:T(8,128)(2,1)}, bf16[4,64,256]{2,1,0:T(8,128)(2,1)S(1)}, u32[]{:S(2)}, u32[]{:S(2)}) collective-permute-start(bf16[4,64,256]{2,1,0:T(8,128)(2,1)} %get-tuple-element.26), channel_id=1, source_target_pairs={{0,6},{1,7},{2,4},{3,5},{4,2},{5,3},{6,0},{7,1},{8,14},{9,15},{10,... | collective-permute-start | bytes 393224 | tf_op jit(solution)/shard_map/ppermute | solution.py:27
  130.3 13.9 %copy-start.16 = (bf16[4,64,256]{2,1,0:T(8,128)(2,1)}, bf16[4,64,256]{2,1,0:T(8,128)(2,1)S(1)}, u32[]{:S(2)}) copy-start(bf16[4,64,256]{2,1,0:T(8,128)(2,1)S(1)} %collective-permute-done.17.refs_6_) | copy-start | bytes 393220
  130.3 17.8 %collective-permute-start.22 = (bf16[4,64,256]{2,1,0:T(8,128)(2,1)}, bf16[4,64,256]{2,1,0:T(8,128)(2,1)S(1)}, u32[]{:S(2)}, u32[]{:S(2)}) collective-permute-start(bf16[4,64,256]{2,1,0:T(8,128)(2,1)} %get-tuple-element.27), channel_id=1, source_target_pairs={{0,7},{1,6},{2,5},{3,4},{4,3},{5,2},{6,1},{7,0},{8,15},{9,14},{10,... | collective-permute-start | bytes 393224 | tf_op jit(solution)/shard_map/ppermute | solution.py:27
  148.1 0.7 copy-start.20
  148.1 0.8 copy-start.21
  157.9 1.0 copy-start
  (5 other events, 3.2 us)
